TPU v7x, 128 devices: a whole 4x4x4 slice. The times are simulated.
128 devices in a mesh: front: 8 (over x, core), grp: 16 (over y, z).
Axes of the slice: x: 4, y: 4, z: 4, core: 2. Of those that a mesh axis runs over, the one named last changes fastest.
Arguments:
- contributions: bfloat16 [16384, 16384], P(('front', 'grp')), may hold values from -6 to 6
- sketch_matrix: bfloat16 [16384, 256], P(('front', 'grp')), may hold values from -0.046875 to 0.046875
- destinations: int32 [16384, 1], replicated, may hold values from 0 to 127; in each aligned block of 128 rows (0 to 127, 128 to 255, ...) at most 2 rows name the same one
- parent_rows: int32 [16384], replicated, may hold values from 0 to 1023
- front_sizes: int32 [8], P('front'), may hold values from 8192 to 16384
- leaf_skeleton: int32 [8, 16, 128], P('front', 'grp'), may hold values from 0 to 1023, as said below
- merge_skeleton: int32 [8, 14, 128], P('front'), may hold values from 0 to 255, as said below
Outputs:
- leaf_maps: float32 [8, 16384, 128], P('front', 'grp')
- node_maps: float32 [8, 16, 3, 256, 128], P('front', 'grp')
- top_rows: float32 [8, 16, 128, 256], P('front', 'grp')
Inputs may be any that keep to these rules, and one draw needn't show every extreme that they name: `destinations`: in the rows of one device no destination is named by more than 2 rows. `leaf_skeleton`: each row holds 128 different row numbers of a leaf block. `merge_skeleton`: each row holds 128 different positions of the stacked 2 * 128 rows.
All inputs are finite; a program needn't handle non-finite values.
Results may differ from a plain program's by a relative error of at most 0.003.
Values may be sent and summed in bfloat16 or wider, within the bound.
No kernel may reach another device: no remote copies, remote signals or barrier semaphores. Data moves between devices by JAX's collectives and lax.ppermute only.
A program may use at most 64 MiB of HBM per device.

v0:
```python
import jax
import jax.numpy as jnp
from jax import lax
from jax.sharding import PartitionSpec as P

PR_DEV = 1024
LEVELS = 3


def from_partner(block, axis, stride):
    count = lax.axis_size(axis)
    route = []
    for low in range(count):
        high = low | 1 << stride
        if high != low and high < count:
            route += [(low, high), (high, low)]
    return lax.ppermute(block, axis, route)


def ridge_map(rows, basis):
    gram = jnp.dot(basis, basis.T, precision=lax.Precision.HIGHEST)
    shift = 0.1 * jnp.mean(jnp.diagonal(gram)) + 1e-05
    ident = jnp.eye(gram.shape[0], dtype=jnp.float32)
    gram = gram + shift * ident
    approx = ident / jnp.trace(gram)
    for step in range(24):
        approx = jnp.dot(
            approx,
            2.0 * ident - jnp.dot(gram, approx, precision=lax.Precision.HIGHEST),
            precision=lax.Precision.HIGHEST,
        )
    right = jnp.dot(rows, basis.T, precision=lax.Precision.HIGHEST)
    return jnp.dot(right, approx, precision=lax.Precision.HIGHEST)


def select_rows(rows, index):
    picker = (index[:, None] == jnp.arange(rows.shape[0], dtype=jnp.int32)[None, :]).astype(
        jnp.float32
    )
    return jnp.dot(picker, rows, precision=lax.Precision.HIGHEST)


def local(
    contributions,
    sketch_matrix,
    destinations,
    parent_rows,
    front_sizes,
    leaf_skeleton,
    merge_skeleton,
):
    fronts = lax.axis_size("front")
    leaves = lax.axis_size("grp")
    devices = fronts * leaves
    grp_index = lax.axis_index("grp")
    myself = lax.axis_index("front") * leaves + grp_index
    rows_dev = contributions.shape[0]
    width = sketch_matrix.shape[1]
    capacity = 2 * rows_dev // devices
    sketch = jnp.dot(
        contributions,
        lax.all_gather(sketch_matrix, ("front", "grp"), axis=0, tiled=True),
        preferred_element_type=jnp.float32,
    )
    sketch = sketch.astype(jnp.bfloat16)
    every_dest = destinations[:, 0].reshape(devices, rows_dev)
    every_row = parent_rows.reshape(devices, rows_dev)
    mine = lax.dynamic_index_in_dim(every_dest, myself, 0, keepdims=False)
    owners = jnp.arange(devices, dtype=jnp.int32)
    hits = (mine[:, None] == owners[None, :]).astype(jnp.int32)
    before = jnp.cumsum(hits, axis=0) - hits
    slot_of = jnp.sum(before * hits, axis=1)
    keys = mine * capacity + slot_of
    placing = (keys[None, :] == jnp.arange(devices * capacity, dtype=jnp.int32)[:, None]).astype(
        jnp.bfloat16
    )
    packed = jnp.dot(placing, sketch, preferred_element_type=jnp.float32).astype(jnp.bfloat16)
    packed = packed.reshape(devices, capacity, width)
    arrived = lax.all_to_all(
        packed, ("front", "grp"), split_axis=0, concat_axis=0, tiled=True
    ).reshape(devices * capacity, width)
    landing = (every_dest == myself).astype(jnp.int32)
    slots = jnp.cumsum(landing, axis=1) - landing
    match = landing[:, None, :] * (
        slots[:, None, :] == jnp.arange(capacity, dtype=jnp.int32)[None, :, None]
    ).astype(jnp.int32)
    local_row = jnp.sum(match * every_row[:, None, :], axis=2)
    filled = jnp.sum(match, axis=2)
    where_to = jnp.where(filled > 0, local_row, -1).reshape(devices * capacity)
    adding = (jnp.arange(PR_DEV, dtype=jnp.int32)[:, None] == where_to[None, :]).astype(
        jnp.bfloat16
    )
    parent = jnp.dot(adding, arrived, preferred_element_type=jnp.float32)
    global_row = grp_index * PR_DEV + jnp.arange(PR_DEV, dtype=jnp.int32)
    parent = jnp.where((global_row < front_sizes[0])[:, None], parent, jnp.zeros_like(parent))
    basis = select_rows(parent, leaf_skeleton[0, 0])
    leaf_map = ridge_map(parent, basis)
    skeletons = merge_skeleton[0]
    level_maps = []
    current = basis
    for level in range(LEVELS):
        partner = from_partner(current, "grp", level)
        upper_side = grp_index >> level & 1 == 1
        first = jnp.where(upper_side, partner, current)
        second = jnp.where(upper_side, current, partner)
        stacked = jnp.concatenate([first, second], axis=0)
        node = leaves - (leaves >> level) + (grp_index >> level + 1)
        chosen = lax.dynamic_index_in_dim(skeletons, node, 0, keepdims=False)
        current = select_rows(stacked, chosen)
        level_maps.append(ridge_map(stacked, current))
    node_maps = jnp.stack(level_maps, axis=0)
    return (leaf_map[None], node_maps[None, None], current[None, None])


def solution(mesh):
    in_specs = (
        P(("front", "grp"), None),
        P(("front", "grp"), None),
        P(),
        P(),
        P("front"),
        P("front", "grp", None),
        P("front", None, None),
    )
    out_specs = (
        P("front", "grp", None),
        P("front", "grp", None, None, None),
        P("front", "grp", None, None),
    )
    return jax.shard_map(local, mesh=mesh, in_specs=in_specs, out_specs=out_specs, check_vma=False)
```

profile of v0, /device:TPU:1, one launch (start us, length us, event | category | flops | bytes accessed | tf_op | source)
XLA Modules:
  0.0 180.9 jit_solution(4281349015124919198)
XLA Ops:
  7.2 0.7 all-gather.2.cloned.1.call-update
  7.9 0.9 copy.16
  9.1 0.7 fusion.47
  11.1 1.0 select_reduce_fusion
  12.1 0.7 fusion.46
  12.8 71.7 %all-gather.2.cloned.1.call-done = bf16[16384,256]{1,0:T(8,128)(2,1)} async-done(((bf16[128,256]{1,0:T(8,128)(2,1)}), bf16[16384,256]{1,0:T(8,128)(2,1)}) %all-gather.2.cloned.1.call-update) | async-done | bytes 8388624 | tf_op jit(solution)/shard_map/all_gather | solution.py:62
  84.5 6.1 %convolution_convert_fusion = bf16[256,256]{1,0:T(8,128)(2,1)S(1)} fusion(bf16[128,16384]{1,0:T(8,128)(2,1)} %param.7, bf16[16384,256]{1,0:T(8,128)(2,1)} %all-gather.2.cloned.1.call-done, s32[128]{0:T(128)S(1)} %fusion.46), kind=kOutput, calls=%fused_computation.102 | convolution fusion | flops 1090650112 | bytes 12714496 | tf_op jit(solution)/shard_map/dot_general | solution.py:77
  90.6 0.7 reshape.69
  91.3 5.4 %all-to-all-start = ((bf16[128,2,256]{2,1,0:T(2,128)(2,1)}), bf16[128,2,256]{2,1,0:T(2,128)(2,1)S(1)}, u32[]{:S(2)}, u32[]{:S(2)}) async-start(bf16[128,2,256]{2,1,0:T(2,128)(2,1)} %reshape.69), calls=%async_computation | async-start | bytes 262144 | tf_op jit(solution)/shard_map/all_to_all | solution.py:79
  97.0 0.7 fusion.43
  97.7 9.0 %all-to-all-done = bf16[128,2,256]{2,1,0:T(2,128)(2,1)S(1)} async-done(((bf16[128,2,256]{2,1,0:T(2,128)(2,1)}), bf16[128,2,256]{2,1,0:T(2,128)(2,1)S(1)}, u32[]{:S(2)}, u32[]{:S(2)}) %all-to-all-start) | async-done | bytes 131104 | tf_op jit(solution)/shard_map/all_to_all | solution.py:79
  106.8 0.3 convolution_select_fusion
  107.1 0.6 fusion.1
  107.7 0.8 collective-permute-start
  108.5 0.3 fusion.63
  108.8 1.0 fusion.62
  109.8 1.2 gather_fusion
  111.0 0.6 reduce_sum.97
  112.3 0.6 select_reduce_fusion.4
  113.6 0.2 select_subtract_fusion.95
  123.8 1.4 convolution_bitcast_fusion
  125.2 0.3 fusion.8
  125.5 0.3 fusion.87
  125.7 0.4 fusion.7
  126.1 1.4 collective-permute-start.1
  127.5 1.2 gather_fusion.1
  128.7 0.6 reduce_sum.99
  130.0 0.6 select_reduce_fusion.3
  131.3 0.2 select_subtract_fusion.71
  141.5 0.3 convolution_bitcast_fusion.3
  141.8 0.3 fusion.6
  142.1 0.3 fusion.111
  142.4 0.4 fusion.5
  142.7 0.7 collective-permute-start.2
  143.5 1.2 gather_fusion.2
  144.7 0.6 reduce_sum.101
  146.0 0.6 select_reduce_fusion.2
  147.3 0.2 select_subtract_fusion.47
  157.5 0.3 convolution_bitcast_fusion.2
  157.8 0.3 fusion.4
  158.1 0.3 fusion.135
  158.3 0.4 fusion.3
  158.7 1.5 gather_fusion.3
  160.3 0.6 reduce_sum.103
  161.5 0.6 select_reduce_fusion.1
  162.8 0.2 select_subtract_fusion.23
  173.0 0.3 convolution_bitcast_fusion.1
  173.3 0.8 maximum_bitcast_fusion
  (213 shorter events, 39.7 us)
Async XLA Ops:
  7.2 100.0 %copy-start.1 = (s32[1,1,128]{2,1,0:T(1,128)S(1)}, s32[1,1,128]{2,1,0:T(1,128)}, u32[]{:S(2)}) copy-start(s32[1,1,128]{2,1,0:T(1,128)} %param.12) | copy-start | bytes 1540
  7.2 77.3 %all-gather.2.cloned.1.call-start = ((), (), s32[]{:S(2)}) async-start(), calls=%async_computation.1 | async-start | bytes 8454144 | tf_op jit(solution)/shard_map/all_gather | solution.py:62
  91.3 15.4 %all-to-all-start = ((bf16[128,2,256]{2,1,0:T(2,128)(2,1)}), bf16[128,2,256]{2,1,0:T(2,128)(2,1)S(1)}, u32[]{:S(2)}, u32[]{:S(2)}) async-start(bf16[128,2,256]{2,1,0:T(2,128)(2,1)} %reshape.69), calls=%async_computation | async-start | bytes 262144 | tf_op jit(solution)/shard_map/all_to_all | solution.py:79
  107.7 17.5 %collective-permute-start = (f32[128,256]{1,0:T(8,128)S(1)}, f32[128,256]{1,0:T(8,128)S(1)}, u32[]{:S(2)}, u32[]{:S(2)}) collective-permute-start(f32[128,256]{1,0:T(8,128)S(1)} %fusion.1), channel_id=1, source_target_pairs={{0,1},{1,0},{2,3},{3,2},{4,5},{5,4},{6,7},{7,6},{8,9},{9,8},{10,11... | collective-permute-start | bytes 393224 | tf_op jit(solution)/shard_map/ppermute | solution.py:17
  126.1 15.7 %collective-permute-start.1 = (f32[128,256]{1,0:T(8,128)S(1)}, f32[128,256]{1,0:T(8,128)S(1)}, u32[]{:S(2)}, u32[]{:S(2)}) collective-permute-start(f32[128,256]{1,0:T(8,128)S(1)} %fusion.8), channel_id=1, source_target_pairs={{0,2},{2,0},{1,3},{3,1},{4,6},{6,4},{5,7},{7,5},{8,10},{10,8},{9,1... | collective-permute-start | bytes 393224 | tf_op jit(solution)/shard_map/ppermute | solution.py:17
  142.7 15.0 %collective-permute-start.2 = (f32[128,256]{1,0:T(8,128)S(1)}, f32[128,256]{1,0:T(8,128)S(1)}, u32[]{:S(2)}, u32[]{:S(2)}) collective-permute-start(f32[128,256]{1,0:T(8,128)S(1)} %fusion.6), channel_id=1, source_target_pairs={{0,4},{4,0},{1,5},{5,1},{2,6},{6,2},{3,7},{7,3},{8,12},{12,8},{9,1... | collective-permute-start | bytes 393224 | tf_op jit(solution)/shard_map/ppermute | solution.py:17
  158.1 16.0 %copy-start = (f32[128,256]{1,0:T(8,128)}, f32[128,256]{1,0:T(8,128)S(1)}, u32[]{:S(2)}) copy-start(f32[128,256]{1,0:T(8,128)S(1)} %fusion.4) | copy-start | bytes 393220
Sparse Core Ops, SparseCore 0:
  11.1 73.3 all-gather.1
where the time goes:
time: 181 us
  waiting for transfers between devices  81.5 us (45%)
  matrix products  52.4 us (29%)
  between operations  21.9 us (12%)
  local copies, waits for them, and re-layouts  8.81 us (5%)
  starting transfers between devices  8.28 us (5%)
  other arithmetic  8.05 us (4%)
    all_gather x1, waiting for transfers between devices, local(): lax.all_gather(sketch_matrix, ('front', 'grp'), axis=0, tiled=True)  71.7 us
    dot_general x96, matrix products, ridge_map(): jnp.dot(gram, approx, precision=lax.Precision.HIGHEST)  19.7 us
    dot_general x96, matrix products, ridge_map(): jnp.dot(approx, 2.0 * ident - jnp.dot(gram, approx, precision=lax.Precisi...  19.5 us
    all_to_all x1, waiting for transfers between devices, local(): lax.all_to_all(packed, ('front', 'grp'), split_axis=0, concat_axis=0, til...  9.02 us
    dot_general x1, matrix products, local(): jnp.dot(placing, sketch, preferred_element_type=jnp.float32)  6.12 us
    all_to_all x1, starting transfers between devices, local(): lax.all_to_all(packed, ('front', 'grp'), split_axis=0, concat_axis=0, til...  5.37 us
    gather x4, local copies, waits for them, and re-layouts, ridge_map(): shift = 0.1 * jnp.mean(jnp.diagonal(gram)) + 1e-05  5.28 us
  transfers between devices with their start and end apart: 5, of which 2 were waited for; matrix products, arithmetic and copies ran while one was open for 25% of the time, Pallas kernels for 0%

commit v1 on v0

--- a/solution.py
+++ b/solution.py
@@ -59,7 +59,12 @@
     capacity = 2 * rows_dev // devices
     sketch = jnp.dot(
         contributions,
-        lax.all_gather(sketch_matrix, ("front", "grp"), axis=0, tiled=True),
+        jnp.concatenate(
+            lax.all_to_all(
+                jnp.stack([sketch_matrix] * lax.axis_size(("front", "grp"))), ("front", "grp"), 0, 0
+            ),
+            axis=0,
+        ),
         preferred_element_type=jnp.float32,
     )
     sketch = sketch.astype(jnp.bfloat16)

time: 181 us -> 217 us (1.20)
  waiting for transfers between devices: 81.5 us -> 113 us
  starting transfers between devices: 8.28 us -> 23.7 us
  between operations: 21.9 us -> 8.56 us
  local copies, waits for them, and re-layouts: 8.81 us -> 12.4 us
    all_to_all x0 -> x1, waiting for transfers between devices: none -> 104 us  [local(): lax.all_to_all(jnp.stack([sketch_matrix] * lax.axis_size(('front', 'grp')...]
    all_gather x1 -> x0, waiting for transfers between devices: 71.7 us -> none  [local(): lax.all_gather(sketch_matrix, ('front', 'grp'), axis=0, tiled=True)]
    all_to_all x0 -> x1, starting transfers between devices: none -> 11.9 us  [local(): lax.all_to_all(jnp.stack([sketch_matrix] * lax.axis_size(('front', 'grp')...]
    another operation x0 -> x1, local copies, waits for them, and re-layouts: none -> 5.09 us  [local(): jnp.stack([sketch_matrix] * lax.axis_size(('front', 'grp')))]
    all_to_all x1, starting transfers between devices: 5.37 us -> 8.89 us  [local(): lax.all_to_all(packed, ('front', 'grp'), split_axis=0, concat_axis=0, til...]
  transfers between devices with their start and end apart: 5 -> 5, of which waited for: 2 -> 2; matrix products, arithmetic and copies ran while one was open for 25% -> 19% of each run, Pallas kernels for 0% -> 0%
where the time goes in v1:
time: 217 us; the launch traced here: 216 us
  waiting for transfers between devices  113 us (52%)
  matrix products  52.4 us (24%)
  starting transfers between devices  23.7 us (11%)
  local copies, waits for them, and re-layouts  12.4 us (6%)
  between operations  8.56 us (4%)
  other arithmetic  6.52 us (3%)
    all_to_all x1, waiting for transfers between devices, local(): lax.all_to_all(jnp.stack([sketch_matrix] * lax.axis_size(('front', 'grp')...  104 us
    dot_general x96, matrix products, ridge_map(): jnp.dot(gram, approx, precision=lax.Precision.HIGHEST)  19.7 us
    dot_general x96, matrix products, ridge_map(): jnp.dot(approx, 2.0 * ident - jnp.dot(gram, approx, precision=lax.Precisi...  19.5 us
    all_to_all x1, starting transfers between devices, local(): lax.all_to_all(jnp.stack([sketch_matrix] * lax.axis_size(('front', 'grp')...  11.9 us
    all_to_all x1, waiting for transfers between devices, local(): lax.all_to_all(packed, ('front', 'grp'), split_axis=0, concat_axis=0, til...  9.02 us
    all_to_all x1, starting transfers between devices, local(): lax.all_to_all(packed, ('front', 'grp'), split_axis=0, concat_axis=0, til...  8.89 us
    dot_general x1, matrix products, local(): jnp.dot(placing, sketch, preferred_element_type=jnp.float32)  6.12 us
    gather x4, local copies, waits for them, and re-layouts, ridge_map(): shift = 0.1 * jnp.mean(jnp.diagonal(gram)) + 1e-05  5.28 us
  transfers between devices with their start and end apart: 5, of which 2 were waited for; matrix products, arithmetic and copies ran while one was open for 19% of the time, Pallas kernels for 0%

profile of v1, /device:TPU:1, one launch (start us, length us, event | category | flops | bytes accessed | tf_op | source)
XLA Modules:
  0.0 216.2 jit_solution(8791549030148630801)
XLA Ops:
  0.6 5.1 %stack.10 = bf16[128,128,256]{2,1,0:T(8,128)(2,1)} broadcast(bf16[128,256]{1,0:T(8,128)(2,1)} %param.8), dimensions={1,2} | broadcast | bytes 8454144 | tf_op jit(solution)/shard_map/stack | solution.py:64
  5.7 11.9 %all-to-all-start = ((bf16[128,128,256]{2,1,0:T(8,128)(2,1)}), bf16[128,128,256]{2,1,0:T(8,128)(2,1)}, u32[]{:S(2)}, u32[]{:S(2)}) async-start(bf16[128,128,256]{2,1,0:T(8,128)(2,1)} %stack.10), calls=%async_computation | async-start | bytes 16777216 | tf_op jit(solution)/shard_map/all_to_all | solution.py:63
  19.5 103.6 %all-to-all-done = bf16[128,128,256]{2,1,0:T(8,128)(2,1)} async-done(((bf16[128,128,256]{2,1,0:T(8,128)(2,1)}), bf16[128,128,256]{2,1,0:T(8,128)(2,1)}, u32[]{:S(2)}, u32[]{:S(2)}) %all-to-all-start) | async-done | bytes 8388640 | tf_op jit(solution)/shard_map/all_to_all | solution.py:63
  123.1 6.1 %convolution_convert_fusion = bf16[256,256]{1,0:T(8,128)(2,1)S(1)} fusion(bf16[128,16384]{1,0:T(8,128)(2,1)} %param.7, bf16[16384,256]{1,0:T(8,128)(2,1)} %bitcast.6, s32[128]{0:T(128)S(1)} %fusion.46), kind=kOutput, calls=%fused_computation.102 | convolution fusion | flops 1090650112 | bytes 12714496 | tf_op jit(solution)/shard_map/dot_general | solution.py:82
  129.2 0.7 reshape.75
  129.9 8.9 %all-to-all-start.1 = ((bf16[128,2,256]{2,1,0:T(2,128)(2,1)}), bf16[128,2,256]{2,1,0:T(2,128)(2,1)S(1)}, u32[]{:S(2)}, u32[]{:S(2)}) async-start(bf16[128,2,256]{2,1,0:T(2,128)(2,1)} %reshape.75), calls=%async_computation.1 | async-start | bytes 262144 | tf_op jit(solution)/shard_map/all_to_all | solution.py:84
  139.1 0.7 fusion.43
  139.8 9.0 %all-to-all-done.1 = bf16[128,2,256]{2,1,0:T(2,128)(2,1)S(1)} async-done(((bf16[128,2,256]{2,1,0:T(2,128)(2,1)}), bf16[128,2,256]{2,1,0:T(2,128)(2,1)S(1)}, u32[]{:S(2)}, u32[]{:S(2)}) %all-to-all-start.1) | async-done | bytes 131104 | tf_op jit(solution)/shard_map/all_to_all | solution.py:84
  148.9 0.3 convolution_select_fusion
  149.2 0.6 fusion.1
  149.8 1.0 fusion.62
  150.8 0.3 fusion.63
  151.1 0.8 collective-permute-start
  151.9 1.2 gather_fusion
  153.1 0.6 reduce_sum.97
  154.4 0.6 select_reduce_fusion.4
  155.7 0.2 select_subtract_fusion.95
  157.0 0.2 select_subtract_fusion.92
  157.8 0.2 select_subtract_fusion.90
  159.9 0.2 select_subtract_fusion.85
  165.9 1.4 convolution_bitcast_fusion
  167.3 0.3 fusion.8
  167.6 1.4 collective-permute-start.1
  168.9 0.4 fusion.7
  169.3 0.3 fusion.87
  169.6 1.2 gather_fusion.1
  170.8 0.6 reduce_sum.99
  172.1 0.6 select_reduce_fusion.3
  173.4 0.2 select_subtract_fusion.71
  183.6 0.3 convolution_bitcast_fusion.3
  183.9 0.3 fusion.6
  184.2 0.7 collective-permute-start.2
  184.9 0.4 fusion.5
  185.3 0.3 fusion.111
  185.5 1.2 gather_fusion.2
  186.8 0.6 reduce_sum.101
  188.1 0.6 select_reduce_fusion.2
  189.4 0.2 select_subtract_fusion.47
  199.6 0.3 convolution_bitcast_fusion.2
  199.9 0.3 fusion.4
  200.2 0.4 fusion.3
  200.5 0.3 fusion.135
  200.8 1.5 gather_fusion.3
  202.4 0.6 reduce_sum.103
  203.6 0.6 select_reduce_fusion.1
  204.9 0.2 select_subtract_fusion.23
  215.1 0.3 convolution_bitcast_fusion.1
  215.4 0.8 maximum_bitcast_fusion
  (217 shorter events, 39.3 us)
Async XLA Ops:
  5.7 12.0 %copy-start.1 = (s32[16384,1]{0,1:T(1,128)S(1)}, s32[16384,1]{0,1:T(1,128)}, u32[]{:S(2)}) copy-start(s32[16384,1]{0,1:T(1,128)} %param.9) | copy-start | bytes 196612
  5.7 13.6 %copy-start.2 = (s32[16384]{0:T(1024)S(1)}, s32[16384]{0:T(1024)}, u32[]{:S(2)}) copy-start(s32[16384]{0:T(1024)} %param.10) | copy-start | bytes 196612
  5.7 117.4 %all-to-all-start = ((bf16[128,128,256]{2,1,0:T(8,128)(2,1)}), bf16[128,128,256]{2,1,0:T(8,128)(2,1)}, u32[]{:S(2)}, u32[]{:S(2)}) async-start(bf16[128,128,256]{2,1,0:T(8,128)(2,1)} %stack.10), calls=%async_computation | async-start | bytes 16777216 | tf_op jit(solution)/shard_map/all_to_all | solution.py:63
  17.7 131.5 %copy-start.3 = (s32[1,1,128]{2,1,0:T(1,128)S(1)}, s32[1,1,128]{2,1,0:T(1,128)}, u32[]{:S(2)}) copy-start(s32[1,1,128]{2,1,0:T(1,128)} %param.12) | copy-start | bytes 1540
  129.9 18.9 %all-to-all-start.1 = ((bf16[128,2,256]{2,1,0:T(2,128)(2,1)}), bf16[128,2,256]{2,1,0:T(2,128)(2,1)S(1)}, u32[]{:S(2)}, u32[]{:S(2)}) async-start(bf16[128,2,256]{2,1,0:T(2,128)(2,1)} %reshape.75), calls=%async_computation.1 | async-start | bytes 262144 | tf_op jit(solution)/shard_map/all_to_all | solution.py:84
  151.1 16.2 %collective-permute-start = (f32[128,256]{1,0:T(8,128)S(1)}, f32[128,256]{1,0:T(8,128)S(1)}, u32[]{:S(2)}, u32[]{:S(2)}) collective-permute-start(f32[128,256]{1,0:T(8,128)S(1)} %fusion.1), channel_id=1, source_target_pairs={{0,1},{1,0},{2,3},{3,2},{4,5},{5,4},{6,7},{7,6},{8,9},{9,8},{10,11... | collective-permute-start | bytes 393224 | tf_op jit(solution)/shard_map/ppermute | solution.py:17
  167.6 16.3 %collective-permute-start.1 = (f32[128,256]{1,0:T(8,128)S(1)}, f32[128,256]{1,0:T(8,128)S(1)}, u32[]{:S(2)}, u32[]{:S(2)}) collective-permute-start(f32[128,256]{1,0:T(8,128)S(1)} %fusion.8), channel_id=1, source_target_pairs={{0,2},{2,0},{1,3},{3,1},{4,6},{6,4},{5,7},{7,5},{8,10},{10,8},{9,1... | collective-permute-start | bytes 393224 | tf_op jit(solution)/shard_map/ppermute | solution.py:17
  184.2 15.7 %collective-permute-start.2 = (f32[128,256]{1,0:T(8,128)S(1)}, f32[128,256]{1,0:T(8,128)S(1)}, u32[]{:S(2)}, u32[]{:S(2)}) collective-permute-start(f32[128,256]{1,0:T(8,128)S(1)} %fusion.6), channel_id=1, source_target_pairs={{0,4},{4,0},{1,5},{5,1},{2,6},{6,2},{3,7},{7,3},{8,12},{12,8},{9,1... | collective-permute-start | bytes 393224 | tf_op jit(solution)/shard_map/ppermute | solution.py:17
  200.1 16.0 %copy-start = (f32[128,256]{1,0:T(8,128)}, f32[128,256]{1,0:T(8,128)S(1)}, u32[]{:S(2)}) copy-start(f32[128,256]{1,0:T(8,128)S(1)} %fusion.4) | copy-start | bytes 393220
